TPU v7x, 128 devices: a whole 4x4x4 slice. The times are simulated.
128 devices in a mesh: leaf: 8 (over x, core), front: 16 (over z, y).
Axes of the slice: x: 4, y: 4, z: 4, core: 2. Of those that a mesh axis runs over, the one named last changes fastest.
Arguments:
- front_matrix: float32 [8, 2048, 2048], P('leaf', 'front'), as said below
- child_blocks: float32 [128, 8, 3, 128, 128], P(('leaf', 'front')), may hold values from -0.046875 to 0.046875
- child_target: int32 [128, 8, 3], P(('leaf', 'front')), may hold values from 0 to 15, as said below
- child_count: int32 [128, 8], P(('leaf', 'front')), may hold values from 1 to 3, as said below
- shot_rhs: float32 [8, 64, 2048], P('leaf'), may hold values from -6 to 6
Outputs:
- factored: float32 [8, 2048, 2048], P('leaf', 'front')
- eliminated: float32 [8, 64, 2048], P('leaf')
Inputs may be any that keep to these rules, and one draw needn't show every extreme that they name: `child_target`: A bucket's code places its block on a row block that the receiving device (leaf index of the bucket, front index of the sender) holds, at a column block no later than that row block. Slots from child_count on are empty and hold no data. In every draw some leaf index receives 3 live blocks from every sender. `front_matrix`: after the child blocks are added, the symmetric matrix that each front's lower triangle defines is positive definite.
All inputs are finite; a program needn't handle non-finite values.
Results may differ from a plain program's by a relative error of at most 0.00013.
Values sent between devices are 32-bit elements; how exact they have to be, the bound alone decides.
No kernel may reach another device: no remote copies, remote signals or barrier semaphores. Data moves between devices by JAX's collectives and lax.ppermute only.
A program may use at most 64 MiB of HBM per device.

v0:
```python
import jax
import jax.numpy as jnp
from jax import lax
from jax.sharding import PartitionSpec as P

BLOCK = 128
PIVOTS = 1024


def spread(value, axis, source):
    kept = jnp.where(lax.axis_index(axis) == source, value, 0).astype(value.dtype)
    return lax.psum(kept, axis)


def lower_sym(square):
    return jnp.tril(square) + jnp.swapaxes(jnp.tril(square, -1), -1, -2)


def right_solve(factor, values):
    solved = jax.scipy.linalg.solve_triangular(factor, jnp.swapaxes(values, 1, 2), lower=True)
    return jnp.swapaxes(solved, 1, 2)


def local(front_matrix, child_blocks, child_target, child_count, shot_rhs):
    fronts_here, rows_local, order_here = front_matrix.shape
    leaf_count = lax.axis_size("leaf")
    capacity = child_blocks.shape[2]
    slot_ids = lax.broadcasted_iota(jnp.int32, child_target.shape, 2)
    live_code = jnp.where(slot_ids < child_count[:, :, None], child_target, -1)
    arrived, codes = (
        lax.all_to_all(child_blocks, "leaf", split_axis=1, concat_axis=1, tiled=True),
        lax.all_to_all(live_code, "leaf", split_axis=1, concat_axis=1, tiled=True),
    )
    count_in = leaf_count * capacity
    flat_blocks = arrived.reshape(count_in, BLOCK * BLOCK)
    flat_codes = codes.reshape(count_in)
    block_cols = order_here // BLOCK
    block_rows = rows_local // BLOCK
    slot_total = fronts_here * block_rows * block_cols
    one_hot = (
        lax.broadcasted_iota(jnp.int32, (slot_total, count_in), 0) == flat_codes[None, :]
    ).astype(jnp.float32)
    summed = jnp.dot(
        one_hot, flat_blocks, precision=lax.Precision.HIGHEST, preferred_element_type=jnp.float32
    )
    extended = summed.reshape(fronts_here, block_rows, block_cols, BLOCK, BLOCK)
    extended = extended.transpose(0, 1, 3, 2, 4).reshape(fronts_here, rows_local, order_here)
    matrix = front_matrix + extended
    my_index = lax.axis_index("front")
    row_global = my_index * rows_local + lax.broadcasted_iota(jnp.int32, (rows_local, 1), 0)
    current_rhs = shot_rhs
    left_parts = []
    diag_parts = []
    solved_parts = []
    for pivot_step in range(PIVOTS // BLOCK):
        start_col = pivot_step * BLOCK
        end_col = start_col + BLOCK
        column_panel = matrix[:, :, start_col:end_col]
        owner_index = start_col // rows_local
        owner_offset = start_col - owner_index * rows_local
        identity_mat = jnp.broadcast_to(jnp.eye(BLOCK, dtype=jnp.float32), column_panel.shape)
        safe_square = jnp.where(my_index == owner_index, lower_sym(column_panel), identity_mat)
        own_factor = jnp.linalg.cholesky(safe_square)
        pivot_factor = spread(own_factor, "front", owner_index)
        my_panel = right_solve(pivot_factor, column_panel)
        my_panel = jnp.where(row_global < start_col, jnp.float32(0.0), my_panel)
        placed = jnp.where(my_index == owner_index, pivot_factor, my_panel)
        my_panel = my_panel.at[:, owner_offset : owner_offset + BLOCK].set(placed)
        full_panel = lax.all_gather(my_panel, "front", axis=1, tiled=True)
        tail_panel = full_panel[:, end_col:]
        update = jnp.einsum(
            "frb,fcb->frc",
            my_panel,
            tail_panel,
            precision=lax.Precision.HIGHEST,
            preferred_element_type=jnp.float32,
        )
        matrix = matrix.at[:, :, end_col:].add(-update)
        zeta = right_solve(pivot_factor, current_rhs[:, :, start_col:end_col])
        rhs_update = jnp.einsum(
            "fnb,fcb->fnc",
            zeta,
            tail_panel,
            precision=lax.Precision.HIGHEST,
            preferred_element_type=jnp.float32,
        )
        current_rhs = current_rhs.at[:, :, end_col:].add(-rhs_update)
        pivots_now = jnp.diagonal(pivot_factor, axis1=1, axis2=2)
        left_parts.append(my_panel / pivots_now[:, None, :])
        diag_parts.append(pivots_now * pivots_now)
        solved_parts.append(zeta * pivots_now[:, None, :])
    col_global = lax.broadcasted_iota(jnp.int32, (1, order_here), 1)
    combined = jnp.concatenate(left_parts + [matrix[:, :, PIVOTS:]], axis=2)
    combined = jnp.where(row_global < col_global, jnp.float32(0.0), combined)
    diag_full = jnp.concatenate(
        diag_parts + [jnp.zeros((fronts_here, order_here - PIVOTS), jnp.float32)], axis=1
    )
    on_diagonal = (row_global == col_global) & (col_global < PIVOTS)
    factored = jnp.where(on_diagonal, diag_full[:, None, :], combined)
    eliminated = jnp.concatenate(solved_parts + [current_rhs[:, :, PIVOTS:]], axis=2)
    return (factored, eliminated)


def solution(mesh):
    return jax.shard_map(
        local,
        mesh=mesh,
        in_specs=(
            P("leaf", "front", None),
            P(("leaf", "front"), None, None, None, None),
            P(("leaf", "front"), None, None),
            P(("leaf", "front"), None),
            P("leaf", None, None),
        ),
        out_specs=(P("leaf", "front", None), P("leaf", None, None)),
        check_vma=False,
    )
```

profile of v0, /device:TPU:0, one launch (start us, length us, event | category | flops | bytes accessed | tf_op | source)
XLA Modules:
  0.0 1286.4 jit_solution(12583845993747838078)
XLA Ops:
  8.6 9.4 all_to_all.10
  18.1 3.6 all-to-all-start.1
  22.0 1.6 copy.269
  24.9 18.3 %all-to-all-done.1 = f32[1,8,3,128,128]{4,3,2,0,1:T(8,128)S(1)} async-done(((f32[1,8,3,128,128]{4,3,2,0,1:T(8,128)}), f32[1,8,3,128,128]{4,3,2,0,1:T(8,128)S(1)}, u32[]{:S(2)}, u32[]{:S(2)}) %all-to-all-start.1) | async-done | bytes 1572896 | tf_op jit(solution)/shard_map/all_to_all | solution.py:31
  43.2 2.6 fusion.31
  45.8 2.6 copy.268
  48.3 1.4 bitcast_add_fusion
  50.1 11.7 custom-call.46
  62.5 1.3 select_select_fusion.8
  63.9 81.6 %all-reduce.9.cloned.1.call-done = f32[1,128,128]{2,1,0:T(8,128)} async-done(((f32[1,128,128]{2,1,0:T(8,128)}), f32[1,128,128]{2,1,0:T(8,128)}) %all-reduce.9.cloned.1.call-update) | async-done | bytes 65552 | tf_op jit(solution)/shard_map/psum | solution.py:12
  146.3 9.8 custom-call.47
  156.1 1.9 gather_fusion
  158.1 1.8 broadcast_divide_fusion.3
  160.2 41.1 %all-gather.9.cloned.1.call-done = f32[1,2048,128]{2,1,0:T(8,128)} async-done(((f32[1,128,128]{2,1,0:T(8,128)}), f32[1,2048,128]{2,1,0:T(8,128)}) %all-gather.9.cloned.1.call-update) | async-done | bytes 1048592 | tf_op jit(solution)/shard_map/all_gather | solution.py:69
  201.3 2.2 fusion.13
  203.9 11.7 custom-call.48
  216.3 1.3 select_select_fusion.7
  217.7 80.3 %all-reduce.11.cloned.1.call-done = f32[1,128,128]{2,1,0:T(8,128)} async-done(((f32[1,128,128]{2,1,0:T(8,128)}), f32[1,128,128]{2,1,0:T(8,128)}) %all-reduce.11.cloned.1.call-update) | async-done | bytes 65552 | tf_op jit(solution)/shard_map/psum | solution.py:12
  298.8 9.8 custom-call.49
  308.6 1.9 gather_fusion.1
  312.1 41.7 %all-gather.11.cloned.1.call-done = f32[1,2048,128]{2,1,0:T(8,128)} async-done(((f32[1,128,128]{2,1,0:T(8,128)}), f32[1,2048,128]{2,1,0:T(8,128)}) %all-gather.11.cloned.1.call-update) | async-done | bytes 1048592 | tf_op jit(solution)/shard_map/all_gather | solution.py:69
  353.8 2.1 fusion.12
  356.3 11.7 custom-call.50
  368.7 1.3 select_select_fusion.6
  370.1 80.3 %all-reduce.13.cloned.1.call-done = f32[1,128,128]{2,1,0:T(8,128)} async-done(((f32[1,128,128]{2,1,0:T(8,128)}), f32[1,128,128]{2,1,0:T(8,128)}) %all-reduce.13.cloned.1.call-update) | async-done | bytes 65552 | tf_op jit(solution)/shard_map/psum | solution.py:12
  451.2 9.8 custom-call.51
  461.1 2.0 gather_fusion.2
  465.9 40.3 %all-gather.13.cloned.1.call-done = f32[1,2048,128]{2,1,0:T(8,128)} async-done(((f32[1,128,128]{2,1,0:T(8,128)}), f32[1,2048,128]{2,1,0:T(8,128)}) %all-gather.13.cloned.1.call-update) | async-done | bytes 1048592 | tf_op jit(solution)/shard_map/all_gather | solution.py:69
  506.3 2.0 fusion.11
  508.6 11.7 custom-call.52
  521.3 1.3 select_select_fusion.5
  523.3 79.7 %all-reduce.15.cloned.1.call-done = f32[1,128,128]{1,2,0:T(8,128)} async-done(((f32[1,128,128]{1,2,0:T(8,128)}), f32[1,128,128]{1,2,0:T(8,128)}) %all-reduce.15.cloned.1.call-update) | async-done | bytes 65552 | tf_op jit(solution)/shard_map/psum | solution.py:12
  603.9 9.8 custom-call.53
  613.7 2.0 gather_fusion.3
  617.3 42.3 %all-gather.15.cloned.1.call-done = f32[1,2048,128]{1,2,0:T(8,128)} async-done(((f32[1,128,128]{1,2,0:T(8,128)}), f32[1,2048,128]{1,2,0:T(8,128)}) %all-gather.15.cloned.1.call-update) | async-done | bytes 1048592 | tf_op jit(solution)/shard_map/all_gather | solution.py:69
  659.6 2.0 fusion.7
  661.9 11.7 custom-call.54
  675.9 80.3 %all-reduce.17.cloned.1.call-done = f32[1,128,128]{1,2,0:T(8,128)} async-done(((f32[1,128,128]{1,2,0:T(8,128)}), f32[1,128,128]{1,2,0:T(8,128)}) %all-reduce.17.cloned.1.call-update) | async-done | bytes 65552 | tf_op jit(solution)/shard_map/psum | solution.py:12
  757.1 9.8 custom-call.55
  766.9 2.0 gather_fusion.4
  770.2 42.6 %all-gather.17.cloned.1.call-done = f32[1,2048,128]{1,2,0:T(8,128)} async-done(((f32[1,128,128]{1,2,0:T(8,128)}), f32[1,2048,128]{1,2,0:T(8,128)}) %all-gather.17.cloned.1.call-update) | async-done | bytes 1048592 | tf_op jit(solution)/shard_map/all_gather | solution.py:69
  812.8 1.9 fusion.5
  815.1 11.7 custom-call.56
  829.0 80.3 %all-reduce.19.cloned.1.call-done = f32[1,128,128]{1,2,0:T(8,128)} async-done(((f32[1,128,128]{1,2,0:T(8,128)}), f32[1,128,128]{1,2,0:T(8,128)}) %all-reduce.19.cloned.1.call-update) | async-done | bytes 65552 | tf_op jit(solution)/shard_map/psum | solution.py:12
  910.2 9.8 custom-call.57
  920.1 2.0 gather_fusion.5
  928.8 37.1 %all-gather.19.cloned.1.call-done = f32[1,2048,128]{1,2,0:T(8,128)} async-done(((f32[1,128,128]{1,2,0:T(8,128)}), f32[1,2048,128]{1,2,0:T(8,128)}) %all-gather.19.cloned.1.call-update) | async-done | bytes 1048592 | tf_op jit(solution)/shard_map/all_gather | solution.py:69
  965.9 1.8 fusion.3
  968.1 11.7 custom-call.58
  982.0 80.3 %all-reduce.21.cloned.1.call-done = f32[1,128,128]{1,2,0:T(8,128)} async-done(((f32[1,128,128]{1,2,0:T(8,128)}), f32[1,128,128]{1,2,0:T(8,128)}) %all-reduce.21.cloned.1.call-update) | async-done | bytes 65552 | tf_op jit(solution)/shard_map/psum | solution.py:12
  1063.3 9.8 custom-call.59
  1073.1 2.0 gather_fusion.6
  1075.1 1.6 divide_dynamic-update-slice_fusion
  1082.5 37.1 %all-gather.21.cloned.1.call-done = f32[1,2048,128]{1,2,0:T(8,128)} async-done(((f32[1,128,128]{1,2,0:T(8,128)}), f32[1,2048,128]{1,2,0:T(8,128)}) %all-gather.21.cloned.1.call-update) | async-done | bytes 1048592 | tf_op jit(solution)/shard_map/all_gather | solution.py:69
  1119.6 2.2 fusion.1
  1122.2 11.7 custom-call.60
  1136.5 1.5 fusion.19
  1138.0 78.5 %all-reduce.23.cloned.1.call-done = f32[1,128,128]{2,1,0:T(8,128)} async-done(((f32[1,128,128]{2,1,0:T(8,128)}), f32[1,128,128]{2,1,0:T(8,128)}) %all-reduce.23.cloned.1.call-update) | async-done | bytes 65552 | tf_op jit(solution)/shard_map/psum | solution.py:12
  1217.4 9.8 custom-call.61
  1227.3 1.9 gather_fusion.7
  1234.3 38.1 %all-gather.23.cloned.1.call-done = f32[1,2048,128]{2,1,0:T(8,128)} async-done(((f32[1,128,128]{2,1,0:T(8,128)}), f32[1,2048,128]{2,1,0:T(8,128)}) %all-gather.23.cloned.1.call-update) | async-done | bytes 1048592 | tf_op jit(solution)/shard_map/all_gather | solution.py:69
  1272.4 2.4 fusion.36
  1274.9 1.7 select_select_fusion
  1276.7 1.3 copy.351
  (244 shorter events, 52.3 us)
Async XLA Ops:
  18.1 25.1 %all-to-all-start.1 = ((f32[1,8,3,128,128]{4,3,2,0,1:T(8,128)}), f32[1,8,3,128,128]{4,3,2,0,1:T(8,128)S(1)}, u32[]{:S(2)}, u32[]{:S(2)}) async-start(f32[1,8,3,128,128]{4,3,2,0,1:T(8,128)} %bitcast.595), calls=%async_computation.1 | async-start | bytes 3145728 | tf_op jit(solution)/shard_map/all_to_all | solution.py:31
  21.7 123.8 %all-reduce.9.cloned.1.call-start = ((), (), s32[]{:S(2)}) async-start(), calls=%async_computation.2 | async-start | bytes 131072 | tf_op jit(solution)/shard_map/psum | solution.py:12
  63.8 137.5 %all-gather.9.cloned.1.call-start = ((), (), s32[]{:S(2)}) async-start(), calls=%async_computation.3 | async-start | bytes 1114112 | tf_op jit(solution)/shard_map/all_gather | solution.py:69
  159.9 138.1 %all-reduce.11.cloned.1.call-start = ((), (), s32[]{:S(2)}) async-start(), calls=%async_computation.4 | async-start | bytes 131072 | tf_op jit(solution)/shard_map/psum | solution.py:12
  217.6 136.2 %all-gather.11.cloned.1.call-start = ((), (), s32[]{:S(2)}) async-start(), calls=%async_computation.5 | async-start | bytes 1114112 | tf_op jit(solution)/shard_map/all_gather | solution.py:69
  311.5 138.8 %all-reduce.13.cloned.1.call-start = ((), (), s32[]{:S(2)}) async-start(), calls=%async_computation.6 | async-start | bytes 131072 | tf_op jit(solution)/shard_map/psum | solution.py:12
  370.0 136.2 %all-gather.13.cloned.1.call-start = ((), (), s32[]{:S(2)}) async-start(), calls=%async_computation.7 | async-start | bytes 1114112 | tf_op jit(solution)/shard_map/all_gather | solution.py:69
  461.0 47.3 %copy-start.16 = (f32[1,128,128]{1,2,0:T(8,128)}, f32[1,128,128]{1,2,0:T(8,128)S(1)}, u32[]{:S(2)}) copy-start(f32[1,128,128]{1,2,0:T(8,128)S(1)} %custom-call.51) | copy-start | bytes 196612
  464.0 139.0 %all-reduce.15.cloned.1.call-start = ((), (), s32[]{:S(2)}) async-start(), calls=%async_computation.8 | async-start | bytes 131072 | tf_op jit(solution)/shard_map/psum | solution.py:12
  522.6 137.0 %all-gather.15.cloned.1.call-start = ((), (), s32[]{:S(2)}) async-start(), calls=%async_computation.9 | async-start | bytes 1114112 | tf_op jit(solution)/shard_map/all_gather | solution.py:69
  613.7 3.6 copy-start.18
  616.7 139.5 %all-reduce.17.cloned.1.call-start = ((), (), s32[]{:S(2)}) async-start(), calls=%async_computation.10 | async-start | bytes 131072 | tf_op jit(solution)/shard_map/psum | solution.py:12
  616.9 42.6 %copy-start.14 = (f32[1,128,128]{1,2,0:T(8,128)S(1)}, f32[1,128,128]{1,2,0:T(8,128)}, u32[]{:S(2)}) copy-start(f32[1,128,128]{1,2,0:T(8,128)} %get-tuple-element.372) | copy-start | bytes 196612
  675.8 137.0 %all-gather.17.cloned.1.call-start = ((), (), s32[]{:S(2)}) async-start(), calls=%async_computation.11 | async-start | bytes 1114112 | tf_op jit(solution)/shard_map/all_gather | solution.py:69
  766.9 47.8 %copy-start.22 = (f32[1,128,128]{1,2,0:T(8,128)}, f32[1,128,128]{1,2,0:T(8,128)S(1)}, u32[]{:S(2)}) copy-start(f32[1,128,128]{1,2,0:T(8,128)S(1)} %custom-call.55) | copy-start | bytes 196612
  769.9 139.4 %all-reduce.19.cloned.1.call-start = ((), (), s32[]{:S(2)}) async-start(), calls=%async_computation.12 | async-start | bytes 131072 | tf_op jit(solution)/shard_map/psum | solution.py:12
  814.7 110.4 %copy-start.15 = (f32[1,64,2048]{2,1,0:T(8,128)S(1)}, f32[1,64,2048]{2,1,0:T(8,128)}, u32[]{:S(2)}) copy-start(f32[1,64,2048]{2,1,0:T(8,128)} %param.78) | copy-start | bytes 1572868
  814.7 111.2 %copy-start = (f32[1,2048,128]{2,1,0:T(8,128)S(1)}, f32[1,2048,128]{2,1,0:T(8,128)}, u32[]{:S(2)}) copy-start(f32[1,2048,128]{2,1,0:T(8,128)} %all-gather.9.cloned.1.call-done) | copy-start | bytes 3145732
  828.9 137.0 %all-gather.19.cloned.1.call-start = ((), (), s32[]{:S(2)}) async-start(), calls=%async_computation.13 | async-start | bytes 1114112 | tf_op jit(solution)/shard_map/all_gather | solution.py:69
  920.0 7.1 copy-start.20
  923.0 42.9 %copy-start.13 = (f32[1,128,128]{1,2,0:T(8,128)S(1)}, f32[1,128,128]{1,2,0:T(8,128)}, u32[]{:S(2)}) copy-start(f32[1,128,128]{1,2,0:T(8,128)} %get-tuple-element.376) | copy-start | bytes 196612
  923.0 139.3 %all-reduce.21.cloned.1.call-start = ((), (), s32[]{:S(2)}) async-start(), calls=%async_computation.14 | async-start | bytes 131072 | tf_op jit(solution)/shard_map/psum | solution.py:12
  927.2 0.8 copy-start.5
  967.7 109.2 %copy-start.1 = (f32[1,2048,128]{2,1,0:T(8,128)S(1)}, f32[1,2048,128]{2,1,0:T(8,128)}, u32[]{:S(2)}) copy-start(f32[1,2048,128]{2,1,0:T(8,128)} %all-gather.11.cloned.1.call-done) | copy-start | bytes 3145732
  967.7 109.2 %copy-start.6 = (f32[1,64,1920]{2,1,0:T(8,128)S(1)}, f32[1,64,1920]{2,1,0:T(8,128)}, u32[]{:S(2)}) copy-start(f32[1,64,1920]{2,1,0:T(8,128)} %copy-done.5) | copy-start | bytes 1474564
  982.0 96.1 %copy-start.17 = (f32[1,128,128]{1,2,0:T(8,128)S(1)}, f32[1,128,128]{1,2,0:T(8,128)}, u32[]{:S(2)}) copy-start(f32[1,128,128]{1,2,0:T(8,128)} %copy-done.16) | copy-start | bytes 196612
  982.0 137.6 %all-gather.21.cloned.1.call-start = ((), (), s32[]{:S(2)}) async-start(), calls=%async_computation.15 | async-start | bytes 1114112 | tf_op jit(solution)/shard_map/all_gather | solution.py:69
  1063.2 15.7 %copy-start.2 = (f32[1,2048,128]{2,1,0:T(8,128)S(1)}, f32[1,2048,128]{2,1,0:T(8,128)}, u32[]{:S(2)}) copy-start(f32[1,2048,128]{2,1,0:T(8,128)} %all-gather.13.cloned.1.call-done) | copy-start | bytes 3145732
  1073.1 3.8 copy-start.24
  1075.1 3.8 copy-start.26
  1076.7 139.9 %all-reduce.23.cloned.1.call-start = ((), (), s32[]{:S(2)}) async-start(), calls=%async_computation.16 | async-start | bytes 131072 | tf_op jit(solution)/shard_map/psum | solution.py:12
  1076.9 3.1 copy-start.19
  1076.9 3.9 copy-start.3
  1078.9 2.5 copy-start.23
  1081.4 0.9 copy-start.8
  1081.4 38.2 %copy-start.11 = (f32[1,128,128]{1,2,0:T(8,128)S(1)}, f32[1,128,128]{1,2,0:T(8,128)}, u32[]{:S(2)}) copy-start(f32[1,128,128]{1,2,0:T(8,128)} %get-tuple-element.378) | copy-start | bytes 196612
  1082.5 54.0 %copy-start.4 = (f32[1,2048,128]{1,2,0:T(8,128)S(1)}, f32[1,2048,128]{1,2,0:T(8,128)}, u32[]{:S(2)}) copy-start(f32[1,2048,128]{1,2,0:T(8,128)} %all-gather.17.cloned.1.call-done) | copy-start | bytes 3145732
  1122.0 107.2 %copy-start.30 = (pred[128]{0:T(512)(128)(4,1)S(1)}, pred[128]{0:T(512)(128)(4,1)}, u32[]{:S(2)}) copy-start(pred[128]{0:T(512)(128)(4,1)} %broadcast_compare_fusion) | copy-start | bytes 388
  1122.1 108.0 %copy-start.21 = (f32[1,128,128]{1,2,0:T(8,128)S(1)}, f32[1,128,128]{1,2,0:T(8,128)}, u32[]{:S(2)}) copy-start(f32[1,128,128]{1,2,0:T(8,128)} %copy-done.20) | copy-start | bytes 196612
  1134.0 97.0 %copy-start.7 = (f32[1,2048,128]{1,2,0:T(8,128)S(1)}, f32[1,2048,128]{1,2,0:T(8,128)}, u32[]{:S(2)}) copy-start(f32[1,2048,128]{1,2,0:T(8,128)} %all-gather.19.cloned.1.call-done) | copy-start | bytes 3145732
  1136.2 136.2 %all-gather.23.cloned.1.call-start = ((), (), s32[]{:S(2)}) async-start(), calls=%async_computation.17 | async-start | bytes 1114112 | tf_op jit(solution)/shard_map/all_gather | solution.py:69
  1138.0 93.4 %copy-start.27 = (f32[128]{0:T(128)S(1)}, f32[128]{0:T(128)}, u32[]{:S(2)}) copy-start(f32[128]{0:T(128)} %copy-done.26) | copy-start | bytes 1540
  1138.0 93.5 %copy-start.25 = (f32[1,128,128]{1,2,0:T(8,128)S(1)}, f32[1,128,128]{1,2,0:T(8,128)}, u32[]{:S(2)}) copy-start(f32[1,128,128]{1,2,0:T(8,128)} %copy-done.24) | copy-start | bytes 196612
  1138.0 94.3 %copy-start.9 = (f32[1,2048,128]{1,2,0:T(8,128)S(1)}, f32[1,2048,128]{1,2,0:T(8,128)}, u32[]{:S(2)}) copy-start(f32[1,2048,128]{1,2,0:T(8,128)} %all-gather.21.cloned.1.call-done) | copy-start | bytes 3145732
  1231.0 41.5 %copy-start.12 = (f32[1,128,128]{2,1,0:T(8,128)S(1)}, f32[1,128,128]{2,1,0:T(8,128)}, u32[]{:S(2)}) copy-start(f32[1,128,128]{2,1,0:T(8,128)} %get-tuple-element.380) | copy-start | bytes 196612
  1232.3 42.6 %copy-start.31 = (s32[128]{0:T(128)S(1)}, s32[128]{0:T(128)}, u32[]{:S(2)}) copy-start(s32[128]{0:T(128)} %iota_add_fusion.1) | copy-start | bytes 1540
  1276.6 1.3 copy-start.10
  1276.6 1.6 copy-start.28
  1278.9 0.8 copy-start.29
Sparse Core Ops, SparseCore 0:
  63.9 81.5 all-reduce.8
  160.0 41.2 all-gather.8
  217.7 80.2 all-reduce.10
  311.7 42.1 all-gather.10
  370.1 80.1 all-reduce.12
  464.1 42.1 all-gather.12
  522.7 80.2 all-reduce.14
  616.8 42.7 all-gather.14
  675.9 80.2 all-reduce.16
  770.0 42.7 all-gather.16
  829.0 80.2 all-reduce.18
  923.1 42.7 all-gather.18
  982.1 80.1 all-reduce.20
  1076.8 42.7 all-gather.20
  1136.3 80.2 all-reduce.22
  1230.3 42.1 all-gather.22
where the time goes:
time: 1300 us; the launch traced here: 1290 us
  waiting for transfers between devices  980 us (75%)
  other arithmetic  202 us (16%)
  matrix products  41.7 us (3%)
  local copies, waits for them, and re-layouts  31.6 us (2%)
  between operations  15.4 us (1%)
    psum x8, waiting for transfers between devices, spread(): return lax.psum(kept, axis)  641 us
    all_gather x8, waiting for transfers between devices, local(): full_panel = lax.all_gather(my_panel, 'front', axis=1, tiled=True)  320 us
    another operation x24, other arithmetic, local(): own_factor = jnp.linalg.cholesky(safe_square)  99.8 us
    another operation x16, other arithmetic, right_solve(): jax.scipy.linalg.solve_triangular(factor, jnp.swapaxes(values, 1, 2), low...  85.3 us
  transfers between devices with their start and end apart: 17, of which 17 were waited for; matrix products, arithmetic and copies ran while one was open for 2% of the time, Pallas kernels for 0%

commit v1 on v0

--- a/solution.py
+++ b/solution.py
@@ -66,7 +66,10 @@
         my_panel = jnp.where(row_global < start_col, jnp.float32(0.0), my_panel)
         placed = jnp.where(my_index == owner_index, pivot_factor, my_panel)
         my_panel = my_panel.at[:, owner_offset : owner_offset + BLOCK].set(placed)
-        full_panel = lax.all_gather(my_panel, "front", axis=1, tiled=True)
+        reached = jnp.stack([my_panel for _ in range(lax.axis_size("front"))], axis=0)
+        full_panel = jnp.concatenate(
+            lax.all_to_all(reached, axis_name="front", split_axis=0, concat_axis=0), axis=1
+        )
         tail_panel = full_panel[:, end_col:]
         update = jnp.einsum(
             "frb,fcb->frc",

time: 1300 us -> 1120 us (0.86)
  waiting for transfers between devices: 980 us -> 737 us
  starting transfers between devices: 6.55 us -> 45.4 us
  local copies, waits for them, and re-layouts: 31.6 us -> 51.3 us
    all_gather x8 -> x0, waiting for transfers between devices: 320 us -> none  [local(): full_panel = lax.all_gather(my_panel, 'front', axis=1, tiled=True)]
    all_to_all x0 -> x8, waiting for transfers between devices: none -> 90.7 us  [local(): lax.all_to_all(reached, axis_name='front', split_axis=0, concat_axis=0)]
    all_to_all x0 -> x8, starting transfers between devices: none -> 39.5 us  [local(): lax.all_to_all(reached, axis_name='front', split_axis=0, concat_axis=0)]
    another operation x4 -> x16, local copies, waits for them, and re-layouts: 0.58 us -> 15.1 us  [the longest x8 9.45 us: local(): jnp.stack([my_panel for _ in range(lax.axis_size('front'))], axis=0)]
    psum x8, waiting for transfers between devices: 641 us -> 627 us  [spread(): return lax.psum(kept, axis)]
  transfers between devices with their start and end apart: 17 -> 17, of which waited for: 17 -> 17; matrix products, arithmetic and copies ran while one was open for 2% -> 4% of each run, Pallas kernels for 0% -> 0%
where the time goes in v1:
time: 1120 us; the launch traced here: 1110 us
  waiting for transfers between devices  737 us (66%)
  other arithmetic  206 us (18%)
  local copies, waits for them, and re-layouts  51.3 us (5%)
  starting transfers between devices  45.4 us (4%)
  matrix products  45.2 us (4%)
  between operations  15.6 us (1%)
    psum x8, waiting for transfers between devices, spread(): return lax.psum(kept, axis)  627 us
    another operation x24, other arithmetic, local(): own_factor = jnp.linalg.cholesky(safe_square)  100 us
    all_to_all x8, waiting for transfers between devices, local(): lax.all_to_all(reached, axis_name='front', split_axis=0, concat_axis=0)  90.7 us
    another operation x16, other arithmetic, right_solve(): jax.scipy.linalg.solve_triangular(factor, jnp.swapaxes(values, 1, 2), low...  86.1 us
    all_to_all x8, starting transfers between devices, local(): lax.all_to_all(reached, axis_name='front', split_axis=0, concat_axis=0)  39.5 us
  transfers between devices with their start and end apart: 17, of which 17 were waited for; matrix products, arithmetic and copies ran while one was open for 4% of the time, Pallas kernels for 0%

profile of v1, /device:TPU:0, one launch (start us, length us, event | category | flops | bytes accessed | tf_op | source)
XLA Modules:
  0.0 1109.3 jit_solution(17455134254913747479)
XLA Ops:
  8.6 9.4 all_to_all.50
  18.1 3.6 all-to-all-start.1
  24.9 18.3 %all-to-all-done.1 = f32[1,8,3,128,128]{4,3,2,0,1:T(8,128)S(1)} async-done(((f32[1,8,3,128,128]{4,3,2,0,1:T(8,128)}), f32[1,8,3,128,128]{4,3,2,0,1:T(8,128)S(1)}, u32[]{:S(2)}, u32[]{:S(2)}) %all-to-all-start.1) | async-done | bytes 1572896 | tf_op jit(solution)/shard_map/all_to_all | solution.py:31
  43.2 2.6 fusion.31
  47.8 11.7 %custom-call.46 = f32[1,128,128]{2,1,0:T(8,128)S(1)} custom-call(f32[1,128,128]{2,1,0:T(8,128)S(1)} %copy.287), custom_call_target="Cholesky" | custom-call | tf_op jit(solution)/shard_map/jit(cholesky)/cholesky | solution.py:63
  61.5 81.7 %all-reduce.9.cloned.1.call-done = f32[1,128,128]{2,1,0:T(8,128)} async-done(((f32[1,128,128]{2,1,0:T(8,128)}), f32[1,128,128]{2,1,0:T(8,128)}) %all-reduce.9.cloned.1.call-update) | async-done | bytes 65552 | tf_op jit(solution)/shard_map/psum | solution.py:12
  144.0 9.8 custom-call.47
  153.9 1.9 gather_fusion
  158.0 4.1 all-to-all-start.2
  162.7 15.2 %all-to-all-done.2 = f32[16,1,128,128]{3,2,1,0:T(8,128)S(1)} async-done(((f32[16,1,128,128]{3,2,1,0:T(8,128)}), f32[16,1,128,128]{3,2,1,0:T(8,128)S(1)}, u32[]{:S(2)}, u32[]{:S(2)}) %all-to-all-start.2) | async-done | bytes 1048608 | tf_op jit(solution)/shard_map/all_to_all | solution.py:71
  179.3 11.7 %custom-call.48 = f32[1,128,128]{2,1,0:T(8,128)S(1)} custom-call(f32[1,128,128]{2,1,0:T(8,128)S(1)} %copy.296), custom_call_target="Cholesky" | custom-call | tf_op jit(solution)/shard_map/jit(cholesky)/cholesky | solution.py:63
  193.0 78.5 %all-reduce.11.cloned.1.call-done = f32[1,128,128]{2,1,0:T(8,128)} async-done(((f32[1,128,128]{2,1,0:T(8,128)}), f32[1,128,128]{2,1,0:T(8,128)}) %all-reduce.11.cloned.1.call-update) | async-done | bytes 65552 | tf_op jit(solution)/shard_map/psum | solution.py:12
  272.4 9.8 custom-call.49
  282.2 1.9 gather_fusion.1
  286.1 5.0 all-to-all-start.3
  291.3 15.6 %all-to-all-done.3 = f32[16,1,128,128]{3,2,1,0:T(8,128)S(1)} async-done(((f32[16,1,128,128]{3,2,1,0:T(8,128)}), f32[16,1,128,128]{3,2,1,0:T(8,128)S(1)}, u32[]{:S(2)}, u32[]{:S(2)}) %all-to-all-start.3) | async-done | bytes 1048608 | tf_op jit(solution)/shard_map/all_to_all | solution.py:71
  306.9 2.1 fusion.12
  309.4 11.7 %custom-call.50 = f32[1,128,128]{2,1,0:T(8,128)S(1)} custom-call(f32[1,128,128]{2,1,0:T(8,128)S(1)} %copy.305), custom_call_target="Cholesky" | custom-call | tf_op jit(solution)/shard_map/jit(cholesky)/cholesky | solution.py:63
  323.1 78.5 %all-reduce.13.cloned.1.call-done = f32[1,128,128]{2,1,0:T(8,128)} async-done(((f32[1,128,128]{2,1,0:T(8,128)}), f32[1,128,128]{2,1,0:T(8,128)}) %all-reduce.13.cloned.1.call-update) | async-done | bytes 65552 | tf_op jit(solution)/shard_map/psum | solution.py:12
  402.5 9.8 custom-call.51
  412.3 1.9 gather_fusion.2
  416.2 5.0 all-to-all-start.4
  427.0 10.0 all-to-all-done.4
  437.0 2.1 fusion.11
  441.8 12.6 %custom-call.52 = f32[1,128,128]{2,1,0:T(8,128)S(1)} custom-call(f32[1,128,128]{2,1,0:T(8,128)} %fusion.92), custom_call_target="Cholesky" | custom-call | tf_op jit(solution)/shard_map/jit(cholesky)/cholesky | solution.py:63
  457.9 77.1 %all-reduce.15.cloned.1.call-done = f32[1,128,128]{1,2,0:T(8,128)} async-done(((f32[1,128,128]{1,2,0:T(8,128)}), f32[1,128,128]{1,2,0:T(8,128)}) %all-reduce.15.cloned.1.call-update) | async-done | bytes 65552 | tf_op jit(solution)/shard_map/psum | solution.py:12
  536.5 10.6 custom-call.53
  547.2 2.0 gather_fusion.3
  549.2 1.8 divide_dynamic-update-slice_fusion.3
  551.7 1.9 stack.19
  553.6 5.0 all-to-all-start.5
  563.2 2.1 slice.716
  565.3 2.3 copy.318
  567.6 6.9 all-to-all-done.5
  574.5 2.3 fusion.7
  578.8 11.7 %custom-call.54 = f32[1,128,128]{2,1,0:T(8,128)S(1)} custom-call(f32[1,128,128]{2,1,0:T(8,128)S(1)} %fusion.88), custom_call_target="Cholesky" | custom-call | tf_op jit(solution)/shard_map/jit(cholesky)/cholesky | solution.py:63
  592.7 78.5 %all-reduce.17.cloned.1.call-done = f32[1,128,128]{1,2,0:T(8,128)} async-done(((f32[1,128,128]{1,2,0:T(8,128)}), f32[1,128,128]{1,2,0:T(8,128)}) %all-reduce.17.cloned.1.call-update) | async-done | bytes 65552 | tf_op jit(solution)/shard_map/psum | solution.py:12
  672.2 9.8 custom-call.55
  682.0 2.0 gather_fusion.4
  686.9 5.0 all-to-all-start.6
  692.4 2.3 fusion.27
  698.2 9.6 all-to-all-done.6
  707.8 2.0 fusion.5
  710.1 11.7 %custom-call.56 = f32[1,128,128]{2,1,0:T(8,128)S(1)} custom-call(f32[1,128,128]{2,1,0:T(8,128)S(1)} %fusion.84), custom_call_target="Cholesky" | custom-call | tf_op jit(solution)/shard_map/jit(cholesky)/cholesky | solution.py:63
  724.0 78.5 %all-reduce.19.cloned.1.call-done = f32[1,128,128]{1,2,0:T(8,128)} async-done(((f32[1,128,128]{1,2,0:T(8,128)}), f32[1,128,128]{1,2,0:T(8,128)}) %all-reduce.19.cloned.1.call-update) | async-done | bytes 65552 | tf_op jit(solution)/shard_map/psum | solution.py:12
  803.4 9.8 custom-call.57
  813.3 2.0 gather_fusion.5
  817.4 5.1 all-to-all-start.7
  824.6 2.1 fusion.21
  826.7 11.6 %all-to-all-done.7 = f32[16,1,128,128]{3,2,1,0:T(8,128)S(1)} async-done(((f32[16,1,128,128]{3,2,1,0:T(8,128)}), f32[16,1,128,128]{3,2,1,0:T(8,128)S(1)}, u32[]{:S(2)}, u32[]{:S(2)}) %all-to-all-start.7) | async-done | bytes 1048608 | tf_op jit(solution)/shard_map/all_to_all | solution.py:71
  839.4 11.7 %custom-call.58 = f32[1,128,128]{2,1,0:T(8,128)S(1)} custom-call(f32[1,128,128]{2,1,0:T(8,128)S(1)} %fusion.80), custom_call_target="Cholesky" | custom-call | tf_op jit(solution)/shard_map/jit(cholesky)/cholesky | solution.py:63
  854.2 77.7 %all-reduce.21.cloned.1.call-done = f32[1,128,128]{1,2,0:T(8,128)} async-done(((f32[1,128,128]{1,2,0:T(8,128)}), f32[1,128,128]{1,2,0:T(8,128)}) %all-reduce.21.cloned.1.call-update) | async-done | bytes 65552 | tf_op jit(solution)/shard_map/psum | solution.py:12
  932.8 9.8 custom-call.59
  942.7 2.0 gather_fusion.6
  946.8 5.1 all-to-all-start.8
  952.2 2.0 fusion.19
  955.4 2.6 fusion.17
  957.9 9.7 all-to-all-done.8
  968.7 11.7 %custom-call.60 = f32[1,128,128]{2,1,0:T(8,128)S(1)} custom-call(f32[1,128,128]{2,1,0:T(8,128)S(1)} %fusion.76), custom_call_target="Cholesky" | custom-call | tf_op jit(solution)/shard_map/jit(cholesky)/cholesky | solution.py:63
  984.2 76.9 %all-reduce.23.cloned.1.call-done = f32[1,128,128]{2,1,0:T(8,128)} async-done(((f32[1,128,128]{2,1,0:T(8,128)}), f32[1,128,128]{2,1,0:T(8,128)}) %all-reduce.23.cloned.1.call-update) | async-done | bytes 65552 | tf_op jit(solution)/shard_map/psum | solution.py:12
  1061.9 9.8 custom-call.61
  1071.7 1.9 gather_fusion.7
  1075.3 5.2 all-to-all-start.9
  1084.2 12.2 %all-to-all-done.9 = f32[16,1,128,128]{3,2,1,0:T(8,128)S(1)} async-done(((f32[16,1,128,128]{3,2,1,0:T(8,128)}), f32[16,1,128,128]{3,2,1,0:T(8,128)S(1)}, u32[]{:S(2)}, u32[]{:S(2)}) %all-to-all-start.9) | async-done | bytes 1048608 | tf_op jit(solution)/shard_map/all_to_all | solution.py:71
  (256 shorter events, 87.3 us)
Async XLA Ops:
  18.1 25.1 %all-to-all-start.1 = ((f32[1,8,3,128,128]{4,3,2,0,1:T(8,128)}), f32[1,8,3,128,128]{4,3,2,0,1:T(8,128)S(1)}, u32[]{:S(2)}, u32[]{:S(2)}) async-start(f32[1,8,3,128,128]{4,3,2,0,1:T(8,128)} %bitcast.615), calls=%async_computation.1 | async-start | bytes 3145728 | tf_op jit(solution)/shard_map/all_to_all | solution.py:31
  21.7 121.5 %all-reduce.9.cloned.1.call-start = ((), (), s32[]{:S(2)}) async-start(), calls=%async_computation.10 | async-start | bytes 131072 | tf_op jit(solution)/shard_map/psum | solution.py:12
  22.0 287.2 %copy-start.11 = (pred[1,128,128]{1,2,0:T(8,128)(4,1)}, pred[1,128,128]{1,2,0:T(8,128)(4,1)S(1)}, u32[]{:S(2)}) copy-start(pred[1,128,128]{1,2,0:T(8,128)(4,1)S(1)} %copy.284) | copy-start | bytes 49156
  158.0 19.9 %all-to-all-start.2 = ((f32[16,1,128,128]{3,2,1,0:T(8,128)}), f32[16,1,128,128]{3,2,1,0:T(8,128)S(1)}, u32[]{:S(2)}, u32[]{:S(2)}) async-start(f32[16,1,128,128]{3,2,1,0:T(8,128)} %stack.16), calls=%async_computation.2 | async-start | bytes 2097152 | tf_op jit(solution)/shard_map/all_to_all | solution.py:71
  162.1 109.4 %all-reduce.11.cloned.1.call-start = ((), (), s32[]{:S(2)}) async-start(), calls=%async_computation.11 | async-start | bytes 131072 | tf_op jit(solution)/shard_map/psum | solution.py:12
  178.9 107.2 %copy-start = (f32[1,128,1920]{1,2,0:T(8,128)}, f32[1,128,1920]{1,2,0:T(8,128)S(1)}, u32[]{:S(2)}) copy-start(f32[1,128,1920]{1,2,0:T(8,128)S(1)} %fusion.13) | copy-start | bytes 2949124
  286.1 20.8 %all-to-all-start.3 = ((f32[16,1,128,128]{3,2,1,0:T(8,128)}), f32[16,1,128,128]{3,2,1,0:T(8,128)S(1)}, u32[]{:S(2)}, u32[]{:S(2)}) async-start(f32[16,1,128,128]{3,2,1,0:T(8,128)} %stack.17), calls=%async_computation.3 | async-start | bytes 2097152 | tf_op jit(solution)/shard_map/all_to_all | solution.py:71
  291.1 110.6 %all-reduce.13.cloned.1.call-start = ((), (), s32[]{:S(2)}) async-start(), calls=%async_computation.12 | async-start | bytes 131072 | tf_op jit(solution)/shard_map/psum | solution.py:12
  309.0 107.2 %copy-start.1 = (f32[1,128,1792]{1,2,0:T(8,128)}, f32[1,128,1792]{1,2,0:T(8,128)S(1)}, u32[]{:S(2)}) copy-start(f32[1,128,1792]{1,2,0:T(8,128)S(1)} %fusion.12) | copy-start | bytes 2752516
  416.2 20.8 %all-to-all-start.4 = ((f32[16,1,128,128]{3,2,1,0:T(8,128)}), f32[16,1,128,128]{3,2,1,0:T(8,128)S(1)}, u32[]{:S(2)}, u32[]{:S(2)}) async-start(f32[16,1,128,128]{3,2,1,0:T(8,128)} %stack.18), calls=%async_computation.4 | async-start | bytes 2097152 | tf_op jit(solution)/shard_map/all_to_all | solution.py:71
  421.2 113.7 %all-reduce.15.cloned.1.call-start = ((), (), s32[]{:S(2)}) async-start(), calls=%async_computation.13 | async-start | bytes 131072 | tf_op jit(solution)/shard_map/psum | solution.py:12
  439.1 0.9 copy-start.2
  547.2 6.4 copy-start.13
  549.2 4.4 copy-start.22
  553.6 20.9 %all-to-all-start.5 = ((f32[16,1,128,128]{3,2,1,0:T(8,128)}), f32[16,1,128,128]{3,2,1,0:T(8,128)}, u32[]{:S(2)}, u32[]{:S(2)}) async-start(f32[16,1,128,128]{3,2,1,0:T(8,128)} %stack.19), calls=%async_computation.5 | async-start | bytes 2097152 | tf_op jit(solution)/shard_map/all_to_all | solution.py:71
  558.6 112.6 %all-reduce.17.cloned.1.call-start = ((), (), s32[]{:S(2)}) async-start(), calls=%async_computation.14 | async-start | bytes 131072 | tf_op jit(solution)/shard_map/psum | solution.py:12
  576.7 0.9 copy-start.3
  682.0 4.9 copy-start.15
  684.0 2.9 copy-start.24
  686.9 20.9 %all-to-all-start.6 = ((f32[16,1,128,128]{3,2,1,0:T(8,128)}), f32[16,1,128,128]{3,2,1,0:T(8,128)}, u32[]{:S(2)}, u32[]{:S(2)}) async-start(f32[16,1,128,128]{3,2,1,0:T(8,128)} %stack.20), calls=%async_computation.6 | async-start | bytes 2097152 | tf_op jit(solution)/shard_map/all_to_all | solution.py:71
  691.9 110.6 %all-reduce.19.cloned.1.call-start = ((), (), s32[]{:S(2)}) async-start(), calls=%async_computation.15 | async-start | bytes 131072 | tf_op jit(solution)/shard_map/psum | solution.py:12
  694.7 13.1 %copy-start.4 = (f32[1,128,1536]{2,1,0:T(8,128)S(1)}, f32[1,128,1536]{2,1,0:T(8,128)}, u32[]{:S(2)}) copy-start(f32[1,128,1536]{2,1,0:T(8,128)} %copy-done.3) | copy-start | bytes 2359300
  696.6 0.8 copy-start.5
  709.7 105.5 %copy-start.34 = (pred[128]{0:T(512)(128)(4,1)S(1)}, pred[128]{0:T(512)(128)(4,1)}, u32[]{:S(2)}) copy-start(pred[128]{0:T(512)(128)(4,1)} %broadcast_compare_fusion.2) | copy-start | bytes 388
  813.3 2.9 copy-start.17
  815.2 1.0 copy-start.27
  816.3 6.4 copy-start.6
  817.4 6.4 copy-start.23
  817.4 6.4 copy-start.14
  817.4 20.9 %all-to-all-start.7 = ((f32[16,1,128,128]{3,2,1,0:T(8,128)}), f32[16,1,128,128]{3,2,1,0:T(8,128)S(1)}, u32[]{:S(2)}, u32[]{:S(2)}) async-start(f32[16,1,128,128]{3,2,1,0:T(8,128)} %stack.21), calls=%async_computation.7 | async-start | bytes 2097152 | tf_op jit(solution)/shard_map/all_to_all | solution.py:71
  822.5 109.4 %all-reduce.21.cloned.1.call-start = ((), (), s32[]{:S(2)}) async-start(), calls=%async_computation.16 | async-start | bytes 131072 | tf_op jit(solution)/shard_map/psum | solution.py:12
  826.7 26.7 %copy-start.7 = (f32[1,64,1536]{2,1,0:T(8,128)}, f32[1,64,1536]{2,1,0:T(8,128)S(1)}, u32[]{:S(2)}) copy-start(f32[1,64,1536]{2,1,0:T(8,128)S(1)} %fusion.21) | copy-start | bytes 1179652
  838.3 15.1 %copy-start.16 = (f32[1,128,128]{1,2,0:T(8,128)S(1)}, f32[1,128,128]{1,2,0:T(8,128)}, u32[]{:S(2)}) copy-start(f32[1,128,128]{1,2,0:T(8,128)} %copy-done.15) | copy-start | bytes 196612
  838.3 15.1 %copy-start.25 = (f32[128]{0:T(128)S(1)}, f32[128]{0:T(128)}, u32[]{:S(2)}) copy-start(f32[128]{0:T(128)} %copy-done.24) | copy-start | bytes 1540
  839.0 105.6 %copy-start.33 = (pred[128]{0:T(512)(128)(4,1)S(1)}, pred[128]{0:T(512)(128)(4,1)}, u32[]{:S(2)}) copy-start(pred[128]{0:T(512)(128)(4,1)} %broadcast_compare_fusion.1) | copy-start | bytes 388
  942.7 4.1 copy-start.19
  944.6 0.9 copy-start.29
  945.7 6.5 copy-start.26
  945.7 6.5 copy-start.8
  946.8 7.5 copy-start.28
  946.8 7.5 copy-start.18
  946.8 20.9 %all-to-all-start.8 = ((f32[16,1,128,128]{3,2,1,0:T(8,128)}), f32[16,1,128,128]{3,2,1,0:T(8,128)S(1)}, u32[]{:S(2)}, u32[]{:S(2)}) async-start(f32[16,1,128,128]{3,2,1,0:T(8,128)} %stack.22), calls=%async_computation.8 | async-start | bytes 2097152 | tf_op jit(solution)/shard_map/all_to_all | solution.py:71
  951.9 109.2 %all-reduce.23.cloned.1.call-start = ((), (), s32[]{:S(2)}) async-start(), calls=%async_computation.17 | async-start | bytes 131072 | tf_op jit(solution)/shard_map/psum | solution.py:12
  954.2 0.9 copy-start.9
  955.4 13.1 %copy-start.12 = (pred[1,128,128]{1,2,0:T(8,128)(4,1)S(1)}, pred[1,128,128]{1,2,0:T(8,128)(4,1)}, u32[]{:S(2)}) copy-start(pred[1,128,128]{1,2,0:T(8,128)(4,1)} %copy-done.11) | copy-start | bytes 49156
  967.7 14.9 %copy-start.20 = (f32[1,128,128]{1,2,0:T(8,128)S(1)}, f32[1,128,128]{1,2,0:T(8,128)}, u32[]{:S(2)}) copy-start(f32[1,128,128]{1,2,0:T(8,128)} %copy-done.19) | copy-start | bytes 196612
  967.7 14.9 %copy-start.30 = (f32[128]{0:T(128)S(1)}, f32[128]{0:T(128)}, u32[]{:S(2)}) copy-start(f32[128]{0:T(128)} %copy-done.29) | copy-start | bytes 1540
  968.3 105.4 %copy-start.32 = (pred[128]{0:T(512)(128)(4,1)S(1)}, pred[128]{0:T(512)(128)(4,1)}, u32[]{:S(2)}) copy-start(pred[128]{0:T(512)(128)(4,1)} %broadcast_compare_fusion) | copy-start | bytes 388
  1073.7 0.5 copy-start.31
  1074.2 6.3 copy-start.10
  1075.3 21.0 %all-to-all-start.9 = ((f32[16,1,128,128]{3,2,1,0:T(8,128)}), f32[16,1,128,128]{3,2,1,0:T(8,128)S(1)}, u32[]{:S(2)}, u32[]{:S(2)}) async-start(f32[16,1,128,128]{3,2,1,0:T(8,128)} %stack.23), calls=%async_computation.9 | async-start | bytes 2097152 | tf_op jit(solution)/shard_map/all_to_all | solution.py:71
  1080.5 17.2 %copy-start.21 = (pred[2048]{0:T(1024)(128)(4,1)S(1)}, pred[2048]{0:T(1024)(128)(4,1)}, u32[]{:S(2)}) copy-start(pred[2048]{0:T(1024)(128)(4,1)} %iota_compare_fusion.8) | copy-start | bytes 6148
  1080.5 17.2 %copy-start.35 = (s32[128]{0:T(128)S(1)}, s32[128]{0:T(128)}, u32[]{:S(2)}) copy-start(s32[128]{0:T(128)} %iota_add_fusion.1) | copy-start | bytes 1540
Sparse Core Ops, SparseCore 0:
  61.6 81.5 all-reduce.8
  193.1 78.3 all-reduce.10
  323.2 78.3 all-reduce.12
  456.5 78.3 all-reduce.14
  592.8 78.3 all-reduce.16
  724.1 78.3 all-reduce.18
  853.5 78.3 all-reduce.20
  982.7 78.3 all-reduce.22
